TPU v7x, 32 devices: a whole 2x2x4 slice. The times are simulated.
32 devices in a mesh: seq: 16 (over z, x, core), tensor: 2 (over y).
Axes of the slice: x: 2, y: 2, z: 4, core: 2. Of those that a mesh axis runs over, the one named last changes fastest.
Arguments:
- hidden: bfloat16 [3072, 4096], P('seq', 'tensor'), may hold values from -170 to 170
- depth: int32 [3072], P('seq'), may hold values from 0 to 4, as said below
- norm_gain: float32 [4096], replicated, may hold values from 0.5 to 2
- w_query: bfloat16 [4096, 2048], P('seq', 'tensor'), may hold values from -2.5 to 2.5
- w_key: bfloat16 [4096, 1024], P('seq', 'tensor'), may hold values from -1 to 1
- w_value: bfloat16 [4096, 1024], P('seq', 'tensor'), may hold values from -0.09375 to 0.09375
- w_out: bfloat16 [2048, 4096], P('tensor', 'seq'), may hold values from -0.1875 to 0.1875
Outputs:
- mixed: bfloat16 [3072, 4096], P('seq', 'tensor')
Inputs may be any that keep to these rules, and one draw needn't show every extreme that they name: A token takes part in this step when its depth exceeds 2. In each aligned block of 192 tokens at most 96 take part, and some block holds exactly 96.
All inputs are finite; a program needn't handle non-finite values.
Results may differ from a plain program's by a relative error of at most 0.015.
Values may be sent and summed in bfloat16 or wider, within the bound.
A program may use at most 64 MiB of HBM per device.

v0:
```python
import jax
import jax.numpy as jnp
from jax import lax
from jax.sharding import PartitionSpec as P

HD = 128
STEP = 2
EPSILON = 1e-05
MASKED_SCORE = -1e30


def block_split(total_rows):
    number = -(-total_rows // 512)
    while total_rows % number != 0:
        number = number + 1
    return number


def online_fold(queries, my_index, slot_width):
    query_rows, kv_heads, group_size, head_size = queries.shape
    query_slot = jnp.arange(query_rows, dtype=jnp.int32)

    def update(running, block):
        row_peak, row_total, weighted = running
        key_block, value_block, flag_block, index_block = block
        scores = jnp.einsum(
            "qjgd,kjd->jgqk", queries, key_block, preferred_element_type=jnp.float32
        ) * head_size ** (-0.5)
        source = index_block // slot_width
        within = index_block % slot_width
        earlier = source[None, :] < my_index
        same_dev = (source[None, :] == my_index) & (within[None, :] <= query_slot[:, None])
        visible = (flag_block[None, :] > 0) & (earlier | same_dev)
        scores = jnp.where(visible[None, None], scores, MASKED_SCORE)
        new_peak = jnp.maximum(row_peak, jnp.max(scores, axis=-1))
        rescale = jnp.exp(row_peak - new_peak)
        expons = jnp.exp(scores - new_peak[..., None])
        row_total = row_total * rescale + jnp.sum(expons, axis=-1)
        weighted = weighted * rescale[..., None] + jnp.einsum(
            "jgqk,kjd->jgqd",
            expons.astype(jnp.bfloat16),
            value_block,
            preferred_element_type=jnp.float32,
        )
        return ((new_peak, row_total, weighted), None)

    def absorb(running, arrived, offset):
        key_rows, value_rows, flag_rows = arrived
        arrived_rows = key_rows.shape[0]
        number = block_split(arrived_rows)
        step_rows = arrived_rows // number
        key_position = jnp.arange(arrived_rows, dtype=jnp.int32)
        shaped = (
            key_rows.reshape(number, step_rows, kv_heads, head_size),
            value_rows.reshape(number, step_rows, kv_heads, head_size),
            flag_rows.reshape(number, step_rows),
            key_position.reshape(number, step_rows),
        )
        running, _ = lax.scan(update, running, shaped)
        return running

    start_state = (
        jnp.full((kv_heads, group_size, query_rows), MASKED_SCORE, jnp.float32),
        jnp.zeros((kv_heads, group_size, query_rows), jnp.float32),
        jnp.zeros((kv_heads, group_size, query_rows, head_size), jnp.float32),
    )
    return (absorb, start_state)


def normalized(running):
    row_peak, row_total, weighted = running
    ratio = weighted / row_total[..., None]
    kv_heads, group_size, query_rows, head_size = ratio.shape
    return (
        jnp.transpose(ratio, (2, 0, 1, 3))
        .reshape(query_rows, kv_heads * group_size * head_size)
        .astype(jnp.bfloat16)
    )


def body(hidden, depth, norm_gain, w_query, w_key, w_value, w_out):
    row_count = hidden.shape[0]
    my_index = lax.axis_index("seq")
    gathered = lax.all_gather(hidden, "tensor", axis=1, tiled=True)
    widened = gathered.astype(jnp.float32)
    inverse = lax.rsqrt(jnp.mean(widened * widened, axis=1, keepdims=True) + EPSILON)
    normed = (widened * inverse * norm_gain[None, :]).astype(jnp.bfloat16)
    arrived = (
        lax.all_gather(w_query, "seq", axis=0, tiled=True),
        lax.all_gather(w_key, "seq", axis=0, tiled=True),
        lax.all_gather(w_value, "seq", axis=0, tiled=True),
    )
    query_sum, key_sum, value_sum = tuple(
        (jnp.dot(normed, matrix, preferred_element_type=jnp.float32) for matrix in arrived)
    )
    kv_heads = w_key.shape[1] // HD
    group_size = w_query.shape[1] // w_key.shape[1]
    queries = query_sum.astype(jnp.bfloat16)
    keys_local = key_sum.astype(jnp.bfloat16)
    values_local = value_sum.astype(jnp.bfloat16)
    living = depth > STEP
    absorb, start_state = online_fold(
        queries.reshape(row_count, kv_heads, group_size, HD), my_index, row_count
    )
    running = absorb(
        start_state,
        (
            lax.all_gather(keys_local, "seq", axis=0, tiled=True),
            lax.all_gather(values_local, "seq", axis=0, tiled=True),
            lax.all_gather(living.astype(jnp.bfloat16), "seq", axis=0, tiled=True),
        ),
        jnp.int32(0),
    )
    attended = normalized(running)
    branch_terms = jnp.dot(
        attended,
        lax.all_gather(w_out, "seq", axis=1, tiled=True),
        preferred_element_type=jnp.float32,
    )
    owned = lax.psum_scatter(
        branch_terms.astype(jnp.bfloat16), "tensor", scatter_dimension=1, tiled=True
    ).astype(jnp.float32)
    return jnp.where(living[:, None], owned, 0.0).astype(jnp.bfloat16)


def solution(mesh):
    return jax.shard_map(
        body,
        mesh=mesh,
        in_specs=(
            P("seq", "tensor"),
            P("seq"),
            P(),
            P("seq", "tensor"),
            P("seq", "tensor"),
            P("seq", "tensor"),
            P("tensor", "seq"),
        ),
        out_specs=P("seq", "tensor"),
        check_vma=False,
    )
```

profile of v0, /device:TPU:0, one launch (start us, length us, event | category | flops | bytes accessed | tf_op | source)
XLA Modules:
  0.0 428.1 jit_solution(162654652320524777)
XLA Ops:
  6.5 0.7 all-gather.8.cloned.1.call-update
  7.3 0.7 all-gather.10.cloned.1.call-update
  8.1 0.7 all-gather.16.cloned.1.call-update
  8.8 30.0 %all-gather.8.cloned.1.call-done = bf16[192,4096]{1,0:T(8,128)(2,1)} async-done(((bf16[192,2048]{1,0:T(8,128)(2,1)}), bf16[192,4096]{1,0:T(8,128)(2,1)}) %all-gather.8.cloned.1.call-update) | async-done | bytes 1572880 | tf_op jit(solution)/shard_map/all_gather | solution.py:84
  38.8 1.8 fusion.22
  40.6 50.7 %all-gather.10.cloned.1.call-done = bf16[4096,512]{1,0:T(8,128)(2,1)} async-done(((bf16[256,512]{1,0:T(8,128)(2,1)}), bf16[4096,512]{1,0:T(8,128)(2,1)}) %all-gather.10.cloned.1.call-update) | async-done | bytes 4194320 | tf_op jit(solution)/shard_map/all_gather | solution.py:90
  91.4 4.4 %convolution_convert_fusion.3 = bf16[192,512]{1,0:T(8,128)(2,1)} fusion(bf16[4096,512]{1,0:T(8,128)(2,1)} %all-gather.10.cloned.1.call-done, bf16[192,4096]{1,0:T(8,128)(2,1)} %all-gather.8.cloned.1.call-done, f32[4096]{0:T(1024)} %param.11, f32[192]{0:T(256)S(1)} %add_rsqrt_fusion), kind=kOutput, calls=%fused_computation.44 | convolution fusion | flops 808550400 | bytes 5980928 | tf_op jit(solution)/shard_map/dot_general | solution.py:94
  95.9 46.6 %all-gather.16.cloned.1.call-done = bf16[4096,512]{1,0:T(8,128)(2,1)} async-done(((bf16[256,512]{1,0:T(8,128)(2,1)}), bf16[4096,512]{1,0:T(8,128)(2,1)}) %all-gather.16.cloned.1.call-update) | async-done | bytes 4194320 | tf_op jit(solution)/shard_map/all_gather | solution.py:91
  142.5 3.9 convolution_convert_fusion.2
  146.5 0.5 all-gather.14.cloned.1.call-update
  147.1 0.7 all-gather.20.cloned.1.call-update
  147.9 0.6 dynamic-slice
  149.2 0.2 dynamic-update-slice
  149.4 32.5 %all-reduce = bf16[3072]{0:T(1024)(128)(2,1)S(1)} all-reduce(bf16[3072]{0:T(1024)(128)(2,1)S(1)} %dynamic-update-slice), channel_id=1, replica_groups=mesh['seq'=16,'tensor'=2] {'seq'}, use_global_device_ids=true, to_apply=%add | all-reduce | flops 3072 | bytes 12288
  181.9 6.7 %all-gather.12.cloned.1.call-done = bf16[3072,512]{1,0:T(8,128)(2,1)} async-done(((bf16[192,512]{1,0:T(8,128)(2,1)}), bf16[3072,512]{1,0:T(8,128)(2,1)}) %all-gather.12.cloned.1.call-update) | async-done | bytes 3145744 | tf_op jit(solution)/shard_map/all_gather | solution.py:108
  188.7 5.5 %reshape.131 = bf16[6,512,4,128]{3,2,1,0:T(4,128)(2,1)} reshape(bf16[3072,512]{1,0:T(8,128)(2,1)} %all-gather.12.cloned.1.call-done) | data formatting | bytes 6291456 | tf_op jit(solution)/shard_map/reshape | solution.py:54
  194.2 40.7 %all-gather.18.cloned.1.call-done = bf16[3072,512]{1,0:T(8,128)(2,1)} async-done(((bf16[192,512]{1,0:T(8,128)(2,1)}), bf16[3072,512]{1,0:T(8,128)(2,1)}) %all-gather.18.cloned.1.call-update) | async-done | bytes 3145744 | tf_op jit(solution)/shard_map/all_gather | solution.py:109
  235.0 5.5 %reshape.133 = bf16[6,512,4,128]{3,2,1,0:T(4,128)(2,1)} reshape(bf16[3072,512]{1,0:T(8,128)(2,1)} %all-gather.18.cloned.1.call-done) | data formatting | bytes 6291456 | tf_op jit(solution)/shard_map/reshape | solution.py:55
  240.5 69.2 %all-gather.14.cloned.1.call-done = bf16[4096,1024]{1,0:T(8,128)(2,1)} async-done(((bf16[256,1024]{1,0:T(8,128)(2,1)}), bf16[4096,1024]{1,0:T(8,128)(2,1)}) %all-gather.14.cloned.1.call-update) | async-done | bytes 8388624 | tf_op jit(solution)/shard_map/all_gather | solution.py:89
  309.6 5.2 %convolution_convert_fusion.1 = bf16[192,1024]{1,0:T(8,128)(2,1)S(1)} fusion(bf16[4096,1024]{1,0:T(8,128)(2,1)} %all-gather.14.cloned.1.call-done, bf16[192,4096]{1,0:T(8,128)(2,1)S(1)} %copy-done.1, f32[4096]{0:T(1024)S(1)} %copy-done.5, f32[192]{0:T(256)S(1)} %add_rsqrt_fusion), kind=kOutput, calls=%fused_computation.42 | convolution fusion | flops 1613955072 | bytes 10371840 | tf_op jit(solution)/shard_map/dot_general | solution.py:94
  314.9 0.3 reshape.132
  315.1 0.8 copy.12
  316.0 46.5 %while.17 = (s32[]{:T(128)}, f32[4,2,192]{2,1,0:T(2,128)S(1)}, f32[4,2,192]{2,1,0:T(2,128)S(1)}, f32[4,2,192,128]{3,2,1,0:T(8,128)}, bf16[6,512]{1,0:T(8,128)(2,...) while((s32[]{:T(128)}, f32[4,2,192]{2,1,0:T(2,128)S(1)}, ...), condition=%wide.region_4.5_spmd.clone, body=%wide.region_1.4_spmd.clone.sunk | while | flops 412303360 | bytes 23443692 | solution.py:59
  316.1 2.4 constant_dynamic-slice_fusion.4
  318.6 1.8 fusion.47
  320.4 1.1 fusion.49
  321.5 0.1 copy-done.2
  321.6 1.2 fusion.51
  322.9 0.9 copy-done.3
  323.9 2.4 constant_dynamic-slice_fusion.4
  326.3 1.8 fusion.47
  328.1 1.1 fusion.49
  329.2 0.1 copy-done.2
  329.4 1.2 fusion.51
  330.6 0.9 copy-done.3
  331.6 2.4 constant_dynamic-slice_fusion.4
  334.0 1.8 fusion.47
  335.8 1.1 fusion.49
  337.1 1.2 fusion.51
  338.3 0.9 copy-done.3
  339.4 2.4 constant_dynamic-slice_fusion.4
  341.7 1.8 fusion.47
  343.5 1.1 fusion.49
  344.7 0.1 copy-done.2
  344.8 1.2 fusion.51
  346.0 0.9 copy-done.3
  347.1 2.4 constant_dynamic-slice_fusion.4
  349.5 1.8 fusion.47
  351.3 1.1 fusion.49
  352.4 0.1 copy-done.2
  352.6 1.2 fusion.51
  353.8 0.9 copy-done.3
  354.8 2.5 constant_dynamic-slice_fusion.4
  357.3 1.8 fusion.47
  359.1 1.1 fusion.49
  360.4 1.2 fusion.51
  361.6 0.9 copy-done.3
  362.5 1.4 fusion.25
  363.9 0.4 copy.14
  364.3 0.3 convert_element_type.50
  364.6 23.6 %all-gather.20.cloned.1.call-done = bf16[1024,4096]{1,0:T(8,128)(2,1)} async-done(((bf16[1024,256]{1,0:T(8,128)(2,1)}), bf16[1024,4096]{1,0:T(8,128)(2,1)}) %all-gather.20.cloned.1.call-update) | async-done | bytes 8388624 | tf_op jit(solution)/shard_map/all_gather | solution.py:117
  388.1 6.4 %convolution_convert_fusion = bf16[192,4096]{1,0:T(8,128)(2,1)} fusion(bf16[192,1024]{1,0:T(8,128)(2,1)S(1)} %convert_element_type.50, bf16[1024,4096]{1,0:T(8,128)(2,1)} %all-gather.20.cloned.1.call-done), kind=kOutput, calls=%fused_computation.35 | convolution fusion | flops 1611399168 | bytes 10354688 | tf_op jit(solution)/shard_map/dot_general | solution.py:115
  394.5 24.5 %reduce-scatter.2.cloned.1.call-done = bf16[192,2048]{1,0:T(8,128)(2,1)} async-done(((bf16[192,4096]{1,0:T(8,128)(2,1)}), bf16[192,2048]{1,0:T(8,128)(2,1)}) %reduce-scatter.2.cloned.1.call-update) | async-done | bytes 786448 | tf_op jit(solution)/shard_map/reduce_scatter | solution.py:120
  419.0 2.2 select_convert_fusion
  (89 shorter events, 1.9 us)
Async XLA Ops:
  6.5 32.3 %all-gather.8.cloned.1.call-start = ((), (), s32[]{:S(2)}) async-start(), calls=%async_computation.1 | async-start | bytes 2359296 | tf_op jit(solution)/shard_map/all_gather | solution.py:84
  7.3 84.1 %all-gather.10.cloned.1.call-start = ((), (), s32[]{:S(2)}) async-start(), calls=%async_computation.2 | async-start | bytes 4456448 | tf_op jit(solution)/shard_map/all_gather | solution.py:90
  8.0 134.5 %all-gather.16.cloned.1.call-start = ((), (), s32[]{:S(2)}) async-start(), calls=%async_computation.5 | async-start | bytes 4456448 | tf_op jit(solution)/shard_map/all_gather | solution.py:91
  8.7 179.9 %all-gather.12.cloned.1.call-start = ((), (), s32[]{:S(2)}) async-start(), calls=%async_computation.3 | async-start | bytes 3342336 | tf_op jit(solution)/shard_map/all_gather | solution.py:108
  40.6 101.9 %copy-start.1 = (bf16[192,4096]{1,0:T(8,128)(2,1)S(1)}, bf16[192,4096]{1,0:T(8,128)(2,1)}, u32[]{:S(2)}) copy-start(bf16[192,4096]{1,0:T(8,128)(2,1)} %all-gather.8.cloned.1.call-done) | copy-start | bytes 4718596
  40.6 101.9 %copy-start.5 = (f32[4096]{0:T(1024)S(1)}, f32[4096]{0:T(1024)}, u32[]{:S(2)}) copy-start(f32[4096]{0:T(1024)} %param.11) | copy-start | bytes 49156
  95.8 52.0 %copy-start.6 = (u32[32]{0:T(128)S(1)}, u32[32]{0:T(128)}, u32[]{:S(2)}) copy-start(u32[32]{0:T(128)} %constant.95) | copy-start | bytes 388
  95.8 53.3 %copy-start.4 = (s32[192]{0:T(256)S(1)}, s32[192]{0:T(256)}, u32[]{:S(2)}) copy-start(s32[192]{0:T(256)} %param.10) | copy-start | bytes 2308
  95.8 139.1 %all-gather.18.cloned.1.call-start = ((), (), s32[]{:S(2)}) async-start(), calls=%async_computation.6 | async-start | bytes 3342336 | tf_op jit(solution)/shard_map/all_gather | solution.py:109
  146.4 163.2 %all-gather.14.cloned.1.call-start = ((), (), s32[]{:S(2)}) async-start(), calls=%async_computation.4 | async-start | bytes 8912896 | tf_op jit(solution)/shard_map/all_gather | solution.py:89
  147.0 241.1 %all-gather.20.cloned.1.call-start = ((), (), s32[]{:S(2)}) async-start(), calls=%async_computation.7 | async-start | bytes 8912896 | tf_op jit(solution)/shard_map/all_gather | solution.py:117
  147.8 271.3 %reduce-scatter.2.cloned.1.call-start = ((), (), s32[]{:S(2)}) async-start(), calls=%async_computation.8 | async-start | bytes 2359296 | tf_op jit(solution)/shard_map/reduce_scatter | solution.py:120
  320.3 1.2 copy-start
  320.3 1.3 copy-start.2
  322.8 0.9 copy-start.3
  328.1 1.2 copy-start
  328.1 1.3 copy-start.2
  330.6 0.9 copy-start.3
  335.8 1.2 copy-start
  335.8 1.3 copy-start.2
  338.3 0.9 copy-start.3
  343.5 1.2 copy-start
  343.5 1.3 copy-start.2
  346.0 0.9 copy-start.3
  351.3 1.2 copy-start
  351.3 1.3 copy-start.2
  353.8 0.9 copy-start.3
  359.1 1.2 copy-start
  359.1 1.3 copy-start.2
  361.6 0.9 copy-start.3
Sparse Core Ops, SparseCore 0:
  8.9 29.8 all-gather.7
  41.0 50.3 all-gather.9
  93.6 48.8 all-gather.15
  144.6 43.9 all-gather.11
  190.8 44.1 all-gather.17
  237.0 72.6 all-gather.13
  311.8 76.2 all-gather.19
  394.7 24.3 reduce-scatter.1
where the time goes:
time: 429 us; the launch traced here: 428 us
  waiting for transfers between devices  295 us (69%)
  matrix products  37.7 us (9%)
  local copies, waits for them, and re-layouts  34.3 us (8%)
  blocking collectives  32.5 us (8%)
  between operations  14.3 us (3%)
  other arithmetic  13.1 us (3%)
    all_gather x1, waiting for transfers between devices, body(): lax.all_gather(w_query, 'seq', axis=0, tiled=True)  69.2 us
    all_gather x1, waiting for transfers between devices, body(): lax.all_gather(w_key, 'seq', axis=0, tiled=True)  50.7 us
    all_gather x1, waiting for transfers between devices, body(): lax.all_gather(w_value, 'seq', axis=0, tiled=True)  46.6 us
    all_gather x1, waiting for transfers between devices, body(): lax.all_gather(values_local, 'seq', axis=0, tiled=True)  40.7 us
    unnamed x1, blocking collectives  32.5 us
    all_gather x1, waiting for transfers between devices, body(): gathered = lax.all_gather(hidden, 'tensor', axis=1, tiled=True)  30 us
    reduce_scatter x1, waiting for transfers between devices, body(): lax.psum_scatter(branch_terms.astype(jnp.bfloat16), 'tensor', scatter_dim...  24.5 us
    all_gather x1, waiting for transfers between devices, body(): lax.all_gather(w_out, 'seq', axis=1, tiled=True)  23.6 us
  transfers between devices with their start and end apart: 8, of which 8 were waited for; matrix products, arithmetic and copies ran while one was open for 16% of the time, Pallas kernels for 0%

commit v1 on v0

--- a/solution.py
+++ b/solution.py
@@ -81,7 +81,7 @@
 def body(hidden, depth, norm_gain, w_query, w_key, w_value, w_out):
     row_count = hidden.shape[0]
     my_index = lax.axis_index("seq")
-    gathered = lax.all_gather(hidden, "tensor", axis=1, tiled=True)
+    gathered = jnp.concatenate(lax.all_gather(hidden, "tensor"), axis=1)
     widened = gathered.astype(jnp.float32)
     inverse = lax.rsqrt(jnp.mean(widened * widened, axis=1, keepdims=True) + EPSILON)
     normed = (widened * inverse * norm_gain[None, :]).astype(jnp.bfloat16)

time: 429 us -> 429 us (level)
  local copies, waits for them, and re-layouts: 34.3 us -> 39.9 us
    all_gather x1, waiting for transfers between devices: 50.7 us -> 45.9 us  [body(): lax.all_gather(w_key, 'seq', axis=0, tiled=True)]
  transfers between devices with their start and end apart: 8 -> 8, of which waited for: 8 -> 8; matrix products, arithmetic and copies ran while one was open for 16% -> 18% of each run, Pallas kernels for 0% -> 0%
where the time goes in v1:
time: 429 us; the launch traced here: 428 us
  waiting for transfers between devices  291 us (68%)
  local copies, waits for them, and re-layouts  39.9 us (9%)
  matrix products  37.5 us (9%)
  blocking collectives  32.7 us (8%)
  between operations  14.3 us (3%)
  other arithmetic  12.3 us (3%)
    all_gather x1, waiting for transfers between devices, body(): lax.all_gather(w_query, 'seq', axis=0, tiled=True)  69.2 us
    all_gather x1, waiting for transfers between devices, body(): lax.all_gather(w_value, 'seq', axis=0, tiled=True)  47.2 us
    all_gather x1, waiting for transfers between devices, body(): lax.all_gather(w_key, 'seq', axis=0, tiled=True)  45.9 us
    all_gather x1, waiting for transfers between devices, body(): lax.all_gather(values_local, 'seq', axis=0, tiled=True)  40.5 us
    unnamed x1, blocking collectives  32.7 us
    all_gather x1, waiting for transfers between devices, body(): gathered = jnp.concatenate(lax.all_gather(hidden, 'tensor'), axis=1)  30 us
    reduce_scatter x1, waiting for transfers between devices, body(): lax.psum_scatter(branch_terms.astype(jnp.bfloat16), 'tensor', scatter_dim...  24.5 us
    all_gather x1, waiting for transfers between devices, body(): lax.all_gather(w_out, 'seq', axis=1, tiled=True)  23.2 us
  transfers between devices with their start and end apart: 8, of which 8 were waited for; matrix products, arithmetic and copies ran while one was open for 18% of the time, Pallas kernels for 0%

profile of v1, /device:TPU:0, one launch (start us, length us, event | category | flops | bytes accessed | tf_op | source)
XLA Modules:
  0.0 428.1 jit_solution(12490174095723024744)
XLA Ops:
  6.5 0.7 all-gather.21.cloned.1.call-update
  7.3 0.7 all-gather.9.cloned.1.call-update
  8.1 0.7 all-gather.15.cloned.1.call-update
  8.8 30.0 %all-gather.21.cloned.1.call-done = bf16[384,2048]{1,0:T(8,128)(2,1)} async-done(((bf16[192,2048]{1,0:T(8,128)(2,1)}), bf16[384,2048]{1,0:T(8,128)(2,1)}) %all-gather.21.cloned.1.call-update) | async-done | bytes 1572880 | tf_op jit(solution)/shard_map/all_gather | solution.py:84
  38.8 3.1 copy.11
  41.9 2.7 copy.20
  44.7 0.4 multiply_reduce_fusion
  45.1 0.4 multiply_convert_fusion
  45.5 45.9 %all-gather.9.cloned.1.call-done = bf16[4096,512]{1,0:T(8,128)(2,1)} async-done(((bf16[256,512]{1,0:T(8,128)(2,1)}), bf16[4096,512]{1,0:T(8,128)(2,1)}) %all-gather.9.cloned.1.call-update) | async-done | bytes 4194320 | tf_op jit(solution)/shard_map/all_gather | solution.py:90
  91.4 3.9 convolution_convert_fusion.3
  95.3 47.2 %all-gather.15.cloned.1.call-done = bf16[4096,512]{1,0:T(8,128)(2,1)} async-done(((bf16[256,512]{1,0:T(8,128)(2,1)}), bf16[4096,512]{1,0:T(8,128)(2,1)}) %all-gather.15.cloned.1.call-update) | async-done | bytes 4194320 | tf_op jit(solution)/shard_map/all_gather | solution.py:91
  142.5 3.8 convolution_convert_fusion.2
  146.4 0.5 all-gather.13.cloned.1.call-update
  147.0 0.7 all-gather.19.cloned.1.call-update
  147.8 0.6 dynamic-slice
  149.1 0.2 dynamic-update-slice
  149.4 32.7 %all-reduce = bf16[3072]{0:T(1024)(128)(2,1)S(1)} all-reduce(bf16[3072]{0:T(1024)(128)(2,1)S(1)} %dynamic-update-slice), channel_id=1, replica_groups=mesh['seq'=16,'tensor'=2] {'seq'}, use_global_device_ids=true, to_apply=%add | all-reduce | flops 3072 | bytes 12288
  182.1 6.7 %all-gather.11.cloned.1.call-done = bf16[3072,512]{1,0:T(8,128)(2,1)} async-done(((bf16[192,512]{1,0:T(8,128)(2,1)}), bf16[3072,512]{1,0:T(8,128)(2,1)}) %all-gather.11.cloned.1.call-update) | async-done | bytes 3145744 | tf_op jit(solution)/shard_map/all_gather | solution.py:108
  188.9 5.5 %reshape.135 = bf16[6,512,4,128]{3,2,1,0:T(4,128)(2,1)} reshape(bf16[3072,512]{1,0:T(8,128)(2,1)} %all-gather.11.cloned.1.call-done) | data formatting | bytes 6291456 | tf_op jit(solution)/shard_map/reshape | solution.py:54
  194.4 40.5 %all-gather.17.cloned.1.call-done = bf16[3072,512]{1,0:T(8,128)(2,1)} async-done(((bf16[192,512]{1,0:T(8,128)(2,1)}), bf16[3072,512]{1,0:T(8,128)(2,1)}) %all-gather.17.cloned.1.call-update) | async-done | bytes 3145744 | tf_op jit(solution)/shard_map/all_gather | solution.py:109
  234.9 5.5 %reshape.137 = bf16[6,512,4,128]{3,2,1,0:T(4,128)(2,1)} reshape(bf16[3072,512]{1,0:T(8,128)(2,1)} %all-gather.17.cloned.1.call-done) | data formatting | bytes 6291456 | tf_op jit(solution)/shard_map/reshape | solution.py:55
  240.5 69.2 %all-gather.13.cloned.1.call-done = bf16[4096,1024]{1,0:T(8,128)(2,1)} async-done(((bf16[256,1024]{1,0:T(8,128)(2,1)}), bf16[4096,1024]{1,0:T(8,128)(2,1)}) %all-gather.13.cloned.1.call-update) | async-done | bytes 8388624 | tf_op jit(solution)/shard_map/all_gather | solution.py:89
  309.6 5.2 %convolution_convert_fusion.1 = bf16[192,1024]{1,0:T(8,128)(2,1)S(1)} fusion(bf16[192,4096]{1,0:T(8,128)(2,1)S(1)} %multiply_convert_fusion, bf16[4096,1024]{1,0:T(8,128)(2,1)} %all-gather.13.cloned.1.call-done), kind=kOutput, calls=%fused_computation.39 | convolution fusion | flops 1610809344 | bytes 10354688 | tf_op jit(solution)/shard_map/dot_general | solution.py:94
  314.9 0.3 reshape.136
  315.1 0.8 copy.13
  316.0 46.8 %while.17 = (s32[]{:T(128)}, f32[4,2,192]{2,1,0:T(2,128)S(1)}, f32[4,2,192]{2,1,0:T(2,128)S(1)}, f32[4,2,192,128]{3,2,1,0:T(8,128)}, bf16[6,512]{1,0:T(8,128)(2,...) while((s32[]{:T(128)}, f32[4,2,192]{2,1,0:T(2,128)S(1)}, ...), condition=%wide.region_4.5_spmd.clone, body=%wide.region_1.4_spmd.clone.sunk | while | flops 412303360 | bytes 23443692 | solution.py:59
  316.2 2.4 constant_dynamic-slice_fusion.4
  318.6 1.8 fusion.44
  320.4 1.1 fusion.46
  321.6 1.3 fusion.48
  322.9 0.9 copy-done.3
  324.0 2.4 constant_dynamic-slice_fusion.4
  326.4 1.8 fusion.44
  328.2 1.1 fusion.46
  329.3 0.1 copy-done.2
  329.4 1.3 fusion.48
  330.7 0.9 copy-done.3
  331.8 2.4 constant_dynamic-slice_fusion.4
  334.2 1.8 fusion.44
  336.0 1.1 fusion.46
  337.2 1.3 fusion.48
  338.5 0.9 copy-done.3
  339.6 2.4 constant_dynamic-slice_fusion.4
  341.9 1.8 fusion.44
  343.7 1.1 fusion.46
  345.0 1.3 fusion.48
  346.3 0.9 copy-done.3
  347.3 2.4 constant_dynamic-slice_fusion.4
  349.8 1.8 fusion.44
  351.6 1.1 fusion.46
  352.8 1.3 fusion.48
  354.1 0.9 copy-done.3
  355.2 2.4 constant_dynamic-slice_fusion.4
  357.6 1.8 fusion.44
  359.4 1.1 fusion.46
  360.6 1.3 fusion.48
  361.9 0.9 copy-done.3
  362.8 1.4 fusion.22
  364.2 0.4 copy.15
  364.6 0.3 convert_element_type.63
  364.9 23.2 %all-gather.19.cloned.1.call-done = bf16[1024,4096]{1,0:T(8,128)(2,1)} async-done(((bf16[1024,256]{1,0:T(8,128)(2,1)}), bf16[1024,4096]{1,0:T(8,128)(2,1)}) %all-gather.19.cloned.1.call-update) | async-done | bytes 8388624 | tf_op jit(solution)/shard_map/all_gather | solution.py:117
  388.1 6.4 %convolution_convert_fusion = bf16[192,4096]{1,0:T(8,128)(2,1)} fusion(bf16[192,1024]{1,0:T(8,128)(2,1)S(1)} %convert_element_type.63, bf16[1024,4096]{1,0:T(8,128)(2,1)} %all-gather.19.cloned.1.call-done), kind=kOutput, calls=%fused_computation.35 | convolution fusion | flops 1611399168 | bytes 10354688 | tf_op jit(solution)/shard_map/dot_general | solution.py:115
  394.5 24.5 %reduce-scatter.2.cloned.1.call-done = bf16[192,2048]{1,0:T(8,128)(2,1)} async-done(((bf16[192,4096]{1,0:T(8,128)(2,1)}), bf16[192,2048]{1,0:T(8,128)(2,1)}) %reduce-scatter.2.cloned.1.call-update) | async-done | bytes 786448 | tf_op jit(solution)/shard_map/reduce_scatter | solution.py:120
  419.0 2.2 select_convert_fusion
  (92 shorter events, 2.2 us)
Async XLA Ops:
  6.5 32.3 %all-gather.21.cloned.1.call-start = ((), (), s32[]{:S(2)}) async-start(), calls=%async_computation.8 | async-start | bytes 2359296 | tf_op jit(solution)/shard_map/all_gather | solution.py:84
  7.3 84.1 %all-gather.9.cloned.1.call-start = ((), (), s32[]{:S(2)}) async-start(), calls=%async_computation.1 | async-start | bytes 4456448 | tf_op jit(solution)/shard_map/all_gather | solution.py:90
  8.0 134.5 %all-gather.15.cloned.1.call-start = ((), (), s32[]{:S(2)}) async-start(), calls=%async_computation.4 | async-start | bytes 4456448 | tf_op jit(solution)/shard_map/all_gather | solution.py:91
  8.7 180.1 %all-gather.11.cloned.1.call-start = ((), (), s32[]{:S(2)}) async-start(), calls=%async_computation.2 | async-start | bytes 3342336 | tf_op jit(solution)/shard_map/all_gather | solution.py:108
  41.9 2.8 copy-start.1
  41.9 3.2 copy-start.4
  95.3 52.5 %copy-start.6 = (u32[32]{0:T(128)S(1)}, u32[32]{0:T(128)}, u32[]{:S(2)}) copy-start(u32[32]{0:T(128)} %constant.95) | copy-start | bytes 388
  95.3 53.8 %copy-start.5 = (s32[192]{0:T(256)S(1)}, s32[192]{0:T(256)}, u32[]{:S(2)}) copy-start(s32[192]{0:T(256)} %param.10) | copy-start | bytes 2308
  95.3 139.7 %all-gather.17.cloned.1.call-start = ((), (), s32[]{:S(2)}) async-start(), calls=%async_computation.5 | async-start | bytes 3342336 | tf_op jit(solution)/shard_map/all_gather | solution.py:109
  146.4 163.3 %all-gather.13.cloned.1.call-start = ((), (), s32[]{:S(2)}) async-start(), calls=%async_computation.3 | async-start | bytes 8912896 | tf_op jit(solution)/shard_map/all_gather | solution.py:89
  147.0 241.2 %all-gather.19.cloned.1.call-start = ((), (), s32[]{:S(2)}) async-start(), calls=%async_computation.6 | async-start | bytes 8912896 | tf_op jit(solution)/shard_map/all_gather | solution.py:117
  147.7 271.3 %reduce-scatter.2.cloned.1.call-start = ((), (), s32[]{:S(2)}) async-start(), calls=%async_computation.7 | async-start | bytes 2359296 | tf_op jit(solution)/shard_map/reduce_scatter | solution.py:120
  320.3 1.2 copy-start
  320.4 1.3 copy-start.2
  322.9 0.9 copy-start.3
  328.1 1.2 copy-start
  328.1 1.3 copy-start.2
  330.7 0.9 copy-start.3
  335.9 1.2 copy-start
  335.9 1.3 copy-start.2
  338.5 0.9 copy-start.3
  343.7 1.2 copy-start
  343.7 1.3 copy-start.2
  346.3 0.9 copy-start.3
  351.5 1.2 copy-start
  351.5 1.3 copy-start.2
  354.1 0.9 copy-start.3
  359.3 1.2 copy-start
  359.3 1.3 copy-start.2
  361.9 0.9 copy-start.3
Sparse Core Ops, SparseCore 0:
  8.9 29.8 all-gather.20
  41.0 50.3 all-gather.8
  93.6 48.8 all-gather.14
  144.6 44.1 all-gather.10
  191.0 43.8 all-gather.16
  237.0 72.6 all-gather.12
  311.8 76.2 all-gather.18
  394.7 24.3 reduce-scatter.1
